TPU v7x, 1024 devices: a whole 8x8x8 slice. The times are simulated.
1024 devices in a mesh: section: 32 (over y_lo, z), dp: 8 (over x), fsdp: 4 (over y_hi, core).
Axes of the slice: x: 8, y: 8 (y_hi: 2, y_lo: 4; y = y_hi * 4 + y_lo), z: 8, core: 2. Of those that a mesh axis runs over, the one named last changes fastest.
Arguments:
- x_down: bfloat16 [32, 8, 512, 6144], P('section', 'dp', 'fsdp'), may hold values from -6 to 6
- x_up: bfloat16 [32, 8, 512, 6144], P('section', 'dp', 'fsdp'), may hold values from -6 to 6
- w_tiles: bfloat16 [32, 2, 20, 2, 128, 128], P('section', None, 'fsdp'), as said below
- tile_rows: int32 [32, 2, 20], P('section'), may hold values from 0 to 47, as said below
- tile_cols: int32 [32, 2, 20], P('section'), may hold values from 0 to 191, as said below
- counts: int32 [32, 2, 4], P('section'), may hold values from 2 to 5, as said below
Outputs:
- tile_grads: bfloat16 [32, 20, 2, 128, 128], P('section', 'fsdp')
Inputs may be any that keep to these rules, and one draw needn't show every extreme that they name: w_tiles[l, 1] equals w_tiles[(l + 16) mod 32, 0]. tile_rows[l, 1] equals tile_rows[(l + 16) mod 32, 0]; the 20 row blocks of one layer are distinct. tile_cols[l, 1] equals tile_cols[(l + 16) mod 32, 0]; every column block that a layer uses is used by exactly two of its slots. counts[l, 1] equals counts[(l + 16) mod 32, 0]; the counts of one layer are the numbers 5 - i * 5 // 4 for i < 4 in some order.
All inputs are finite; a program needn't handle non-finite values.
Results may differ from a plain program's by a relative error of at most 0.0065.
Values may be sent and summed in bfloat16 or wider, within the bound.
A program may use at most 64 MiB of HBM per device.

v0:
```python
import math

import jax
import jax.numpy as jnp
from jax import lax
from jax.sharding import PartitionSpec as P

TILE = 128


tanh_scale = math.sqrt(2.0 / math.pi)
cubic_coef = 0.044715


def shifted(array, axis, by):
    size = lax.axis_size(axis)
    return lax.ppermute(array, axis, [(i, (i + by) % size) for i in range(size)])


def gelu_pair(hidden):
    inner = tanh_scale * (hidden + cubic_coef * hidden * hidden * hidden)
    tangent = jnp.tanh(inner)
    value = 0.5 * hidden * (1.0 + tangent)
    slope = 0.5 * (1.0 + tangent) + 0.5 * hidden * (1.0 - tangent * tangent) * tanh_scale * (
        1.0 + 3.0 * cubic_coef * hidden * hidden
    )
    return (value, slope)


def slot_masks(col_ids, counts_in):
    slots = col_ids.shape[0]
    owners = counts_in.shape[0]
    per_owner = slots // owners
    slot_ids = jnp.arange(slots, dtype=jnp.int32)
    owner_ids = slot_ids // per_owner
    per_slot = jnp.sum(
        jnp.where(
            owner_ids[:, None] == jnp.arange(owners, dtype=jnp.int32)[None, :],
            counts_in[None, :],
            0,
        ),
        axis=1,
    )
    living = slot_ids % per_owner < per_slot
    shared = (col_ids[:, None] == col_ids[None, :]) & living[:, None] & living[None, :]
    return shared.astype(jnp.float32)


def pick_blocks(inputs, row_ids):
    return inputs.reshape(inputs.shape[0], -1, TILE)[:, row_ids]


def block_term(blocks, weights, shared, loss_scale):
    high = lax.Precision.HIGHEST
    contrib = jnp.einsum("nsu,suv->nsv", blocks, weights[:, 0], preferred_element_type=jnp.float32)
    hidden = jnp.einsum("st,ntv->nsv", shared, contrib, precision=high)
    value, slope = gelu_pair(hidden)
    active = value.astype(jnp.bfloat16)
    delta = jnp.einsum("nsu,suv->nsv", active, weights[:, 1], preferred_element_type=jnp.float32)
    cotangent = (loss_scale * (blocks.astype(jnp.float32) + delta)).astype(jnp.bfloat16)
    spread = jnp.einsum(
        "nsv,suv->nsu", cotangent, weights[:, 1], preferred_element_type=jnp.float32
    )
    grad_act = jnp.einsum("st,ntu->nsu", shared, spread, precision=high)
    grad_pre = (grad_act * slope).astype(jnp.bfloat16)
    grad_first = jnp.einsum("nsu,nsv->suv", blocks, grad_pre, preferred_element_type=jnp.float32)
    grad_second = jnp.einsum("nsu,nsv->suv", active, cotangent, preferred_element_type=jnp.float32)
    return jnp.stack([grad_first, grad_second], axis=1).astype(jnp.bfloat16)


def body(x_down, x_up, w_tiles, tile_rows, tile_cols, counts):
    gathered = lax.all_gather(w_tiles, "fsdp", axis=2, tiled=True)
    rows_here = x_down.shape[2]
    loss_scale = float(2 * rows_here * lax.axis_size("dp") * lax.axis_size("fsdp")) ** (-0.5)
    own_mask = slot_masks(tile_cols[0, 0], counts[0, 0])
    own_terms = block_term(
        pick_blocks(x_down[0, 0], tile_rows[0, 0]), gathered[0, 0], own_mask, loss_scale
    )
    mirror_by = lax.axis_size("section") // 2
    partner_terms = block_term(
        pick_blocks(x_up[0, 0], tile_rows[0, 1]),
        gathered[0, 1],
        slot_masks(tile_cols[0, 1], counts[0, 1]),
        loss_scale,
    )
    arrived = shifted(partner_terms, "section", mirror_by)
    summed = own_terms.astype(jnp.float32) + arrived.astype(jnp.float32)
    share = lax.psum_scatter(summed, "fsdp", scatter_dimension=0, tiled=True)
    reduced = lax.psum(share, "dp")
    return reduced.astype(jnp.bfloat16)[None]


def solution(mesh):
    in_specs = (
        P("section", "dp", "fsdp", None),
        P("section", "dp", "fsdp", None),
        P("section", None, "fsdp", None, None, None),
        P("section", None, None),
        P("section", None, None),
        P("section", None, None),
    )
    out_specs = P("section", "fsdp", None, None, None)
    return jax.shard_map(body, mesh=mesh, in_specs=in_specs, out_specs=out_specs, check_vma=False)
```

profile of v0, /device:TPU:22, one launch (start us, length us, event | category | flops | bytes accessed | tf_op | source)
XLA Modules:
  0.0 318.3 jit_solution(7715146632669095639)
XLA Ops:
  6.5 0.0 copy-start
  6.5 0.0 all-gather.2.cloned.1.call-start
  6.5 2.1 copy.83
  8.7 0.0 all-gather.2.cloned.1.call-update
  8.7 0.0 all-reduce.4.cloned.1.call-start
  8.7 0.0 copy-done
  8.7 0.9 copy.90
  9.6 1.6 copy.91
  11.2 1.9 copy.81
  13.1 0.0 copy-start.1
  13.2 0.9 copy.82
  14.1 0.0 copy-done.1
  14.1 0.0 copy-start.2
  14.1 0.0 copy-start.3
  14.1 2.1 gather_fusion.1
  16.2 0.7 gather_fusion
  16.9 0.0 copy-done.2
  17.0 0.1 select_reduce_fusion.1
  17.0 0.0 copy-done.3
  17.1 57.3 %all-gather.2.cloned.1.call-done = bf16[1,2,20,2,128,128]{5,4,2,3,1,0:T(8,128)(2,1)} async-done(((bf16[1,2,5,2,128,128]{5,4,2,3,1,0:T(8,128)(2,1)}), bf16[1,2,20,2,128,128]{5,4,2,3,1,0:T(8,128)(2,1)}) %all-gather.2.cloned.1.call-update) | async-done | bytes 2621456 | tf_op jit(solution)/shard_map/all_gather | solution.py:72
  74.4 1.9 slice_bitcast_fusion.1
  76.3 0.3 convolution_bitcast_fusion.2
  76.6 1.6 fusion.2
  78.3 0.7 fusion.12
  78.9 0.6 convolution_bitcast_fusion
  79.5 0.7 fusion.31
  80.2 1.7 fusion
  81.8 1.2 fusion.30
  83.0 0.1 pad_maximum_fusion
  83.2 2.1 collective-permute-start
  85.3 0.3 convolution_bitcast_fusion.5
  85.6 1.6 fusion.6
  87.3 0.7 fusion.13
  87.9 0.7 fusion.29
  88.6 0.6 convolution_bitcast_fusion.3
  89.2 1.6 fusion.4
  90.8 1.2 fusion.28
  92.0 49.9 %collective-permute-done = bf16[20,2,128,128]{3,2,0,1:T(8,128)(2,1)S(1)} collective-permute-done((bf16[20,2,128,128]{3,2,0,1:T(8,128)(2,1)S(1)}, bf16[20,2,128,128]{3,2,0,1:T(8,128)(2,1)S(1)}, u32[]{:S(2)}, u32[]{:S(2)}) %collective-permute-start) | collective-permute-done | bytes 1310752 | tf_op jit(solution)/shard_map/ppermute | solution.py:17
  141.9 2.0 convert_add_fusion
  143.9 0.0 all-reduce.4.cloned.1.call-update
  143.9 1.3 dynamic-slice
  145.8 127.0 %all-reduce.4.cloned.1.call-done = f32[20,2,128,128]{3,2,0,1:T(8,128)} async-done(((f32[20,2,128,128]{3,2,0,1:T(8,128)}), f32[20,2,128,128]{3,2,0,1:T(8,128)}) %all-reduce.4.cloned.1.call-update) | async-done | bytes 2621456
  272.8 1.1 constant_dynamic-slice_fusion
  274.0 36.8 %all-reduce.5 = bf16[5,2,128,128]{3,2,0,1:T(8,128)(2,1)S(1)} all-reduce(f32[5,2,128,128]{3,2,0,1:T(8,128)S(1)} %constant_dynamic-slice_fusion), channel_id=1, replica_groups=mesh['section'=32,'dp'=8,'fsdp'=4] {'dp'}, use_global_device_ids=true, to_apply=%region_3.4 | all-reduce | flops 163840 | bytes 983040 | tf_op jit(solution)/shard_map/psum | solution.py:89
  310.8 0.7 copy.98
  (6 shorter events, 0.0 us)
Async XLA Ops:
  6.5 2.2 copy-start
  6.5 67.8 %all-gather.2.cloned.1.call-start = ((), (), s32[]{:S(2)}) async-start(), calls=%async_computation | async-start | bytes 3276800 | tf_op jit(solution)/shard_map/all_gather | solution.py:72
  8.7 264.2 %all-reduce.4.cloned.1.call-start = ((), (), s32[]{:S(2)}) async-start(), calls=%async_computation.1 | async-start | bytes 5242880
  13.1 0.9 copy-start.1
  14.1 2.8 copy-start.2
  14.1 2.9 copy-start.3
  83.2 58.7 %collective-permute-start = (bf16[20,2,128,128]{3,2,0,1:T(8,128)(2,1)S(1)}, bf16[20,2,128,128]{3,2,0,1:T(8,128)(2,1)S(1)}, u32[]{:S(2)}, u32[]{:S(2)}) collective-permute-start(bf16[20,2,128,128]{3,2,0,1:T(8,128)(2,1)S(1)} %pad_maximum_fusion), channel_id=1, source_target_pairs={{0,512},{32,544},{64,576},{96,608},{128,640},{160,672},{192,704},{... | collective-permute-start | bytes 3932168 | tf_op jit(solution)/shard_map/ppermute | solution.py:17
Sparse Core Ops, SparseCore 0:
  10.0 64.3 all-gather.1
  144.0 128.7 all-reduce.3
where the time goes:
time: 319 us; the launch traced here: 318 us
  waiting for transfers between devices  234 us (73%)
  blocking collectives  36.8 us (12%)
  local copies, waits for them, and re-layouts  15.2 us (5%)
  between operations  14.3 us (4%)
  matrix products  13.4 us (4%)
    unnamed x3, waiting for transfers between devices  127 us
    all_gather x1, waiting for transfers between devices, body(): gathered = lax.all_gather(w_tiles, 'fsdp', axis=2, tiled=True)  57.3 us
    ppermute x1, waiting for transfers between devices, shifted(): lax.ppermute(array, axis, [(i, (i + by) % size) for i in range(size)])  49.9 us
    psum x1, blocking collectives, body(): reduced = lax.psum(share, 'dp')  36.8 us
    unnamed x13, local copies, waits for them, and re-layouts  7.35 us
  transfers between devices with their start and end apart: 3, of which 3 were waited for; matrix products, arithmetic and copies ran while one was open for 5% of the time, Pallas kernels for 0%

commit v1 on v0

v1 whole, which is shorter than its diff:
```python
import functools
import math

import jax
import jax.numpy as jnp
from jax import lax
from jax.experimental import pallas as pl
from jax.experimental.pallas import tpu as pltpu
from jax.sharding import PartitionSpec as P

TILE = 128
MESH = pl.DeviceIdType.MESH
WAVES = 2

tanh_scale = math.sqrt(2.0 / math.pi)
cubic_coef = 0.044715


def gelu_pair(hidden):
    inner = tanh_scale * (hidden + cubic_coef * hidden * hidden * hidden)
    tangent = jnp.tanh(inner)
    value = 0.5 * hidden * (1.0 + tangent)
    slope = 0.5 * (1.0 + tangent) + 0.5 * hidden * (1.0 - tangent * tangent) * tanh_scale * (
        1.0 + 3.0 * cubic_coef * hidden * hidden
    )
    return value, slope


def dot(a, b, ca, cb):
    return lax.dot_general(a, b, (((ca,), (cb,)), ((), ())), preferred_element_type=jnp.float32)


def slot_pairs(cols, counts):
    slots = cols.shape[1]
    per_owner = slots // counts.shape[1]
    ids = jnp.arange(slots, dtype=jnp.int32)
    live = (jnp.arange(per_owner, dtype=jnp.int32) < counts[:, :, None]).astype(jnp.int32).reshape(cols.shape)
    same = (cols[:, :, None] == cols[:, None, :]) & (ids[:, None] != ids[None, :])
    pair = jnp.sum(jnp.where(same, ids, 0), axis=2)
    other_live = jnp.sum(jnp.where(same, live[:, None, :], 0), axis=2)
    return pair, live, other_live


def pick(rows_s, x_down, x_up, out, sems):
    copies = []
    for layer, x in enumerate((x_down, x_up)):
        for s in range(out.shape[1]):
            at = pl.ds(pl.multiple_of(rows_s[layer, s] * TILE, TILE), TILE)
            copies.append(pltpu.make_async_copy(x.at[:, at], out.at[layer, s], sems.at[layer, s]))
            copies[-1].start()
    for copy in copies:
        copy.wait()


class Links:
    def __init__(self, send_sems, recv_sems):
        self.send_sems, self.recv_sems = send_sems, recv_sems
        self.started = []

    def start(self, src, dst, device):
        i = len(self.started)
        copy = pltpu.make_async_remote_copy(
            src_ref=src, dst_ref=dst, send_sem=self.send_sems.at[i], recv_sem=self.recv_sems.at[i],
            device_id=device, device_id_type=MESH,
        )
        copy.start()
        self.started.append((copy, device))
        return i

    def arrived(self, i, landing):
        device = self.started[i][1]
        pltpu.make_async_remote_copy(
            src_ref=landing, dst_ref=landing, send_sem=self.send_sems.at[i],
            recv_sem=self.recv_sems.at[i], device_id=device, device_id_type=MESH,
        ).wait_recv()

    def drain(self):
        for copy, _ in self.started:
            copy.wait_send()


def copies_of(nx):
    half = nx // 2
    return 2 * (1 + 1 + 1 + 2 + 2 + 2 + 2) + 4 + 2 * WAVES * 2 * (2 * (half - 1) + 1) + 3 * WAVES + WAVES * (nx - 1)


def kernel(nx, ns, loss_scale, pair_s, live_s, both_s, x, w, out,
           xv, wv, ct, sp, sl, gmine, gsend, grecv, gsum, slots_p, slots_m, ysend, yrecv, fin, outv,
           lsem, send_sems, recv_sems):
    f32, bf16 = jnp.float32, jnp.bfloat16
    half = nx // 2
    per_owner = w.shape[1] // (2 * TILE)
    big = w.shape[1]
    chunk_rows = big // nx
    sub = chunk_rows // WAVES
    quarter = big // 4

    me = lax.axis_index("dp")
    sec = lax.axis_index("section")
    own = lax.axis_index("fsdp")
    hi, core = own // 2, own % 2
    right = {"dp": lax.rem(me + 1, nx)}
    left = {"dp": lax.rem(me + nx - 1, nx)}
    mirror = lax.rem(sec + ns // 2, ns)
    across = lax.rem(own + 2, 4)
    sib = {"fsdp": own + 1 - 2 * core}
    y_same = {"section": mirror}
    y_cross = {"section": mirror, "fsdp": across}
    y_far = {"fsdp": across}
    peers = (right, left, sib, y_cross, y_same, y_far)

    loads = [
        pltpu.make_async_copy(w, wv.at[:, 0, 0], lsem.at[0]),
        pltpu.make_async_copy(x, xv, lsem.at[1]),
    ]
    for load in loads:
        load.start()

    barrier = pltpu.get_barrier_semaphore()
    for peer in peers:
        pl.semaphore_signal(barrier, inc=1, device_id=peer, device_id_type=MESH)
    pl.semaphore_wait(barrier, len(peers))

    links = Links(send_sems, recv_sems)

    def quart(x):
        return pl.ds(pl.multiple_of(lax.rem(x, 4) * quarter, quarter), quarter)

    def halfq(x, second):
        return pl.ds(pl.multiple_of(lax.rem(x, 4) * quarter + second * (quarter // 2), quarter // 2), quarter // 2)

    q_me, q_left, q_right = quart(me), quart(me + 3), quart(me + 1)
    q_far0, q_far1 = halfq(me + 2, 0), halfq(me + 2, 1)

    c_y, c_sib = [], []
    for layer in range(2):
        c_y.append(links.start(w.at[1 - layer, q_me], wv.at[layer, 1, 0, q_me], y_cross))
    for layer in range(2):
        c_sib.append([links.start(w.at[layer], wv.at[layer, 0, 1], sib)])

    def slot_of(k, cr, j):
        return (lax.rem(hi + k, 2) * 2 + lax.rem(core + cr, 2)) * per_owner + j

    c_r, c_l, c_fr, c_fl = [], [], [], []
    for layer in range(2):
        wc = wv.at[layer, 1, 0]
        links.arrived(c_y[layer], wc.at[q_me])
        c_r.append(links.start(wc.at[q_me], wc.at[q_me], right))
        c_l.append(links.start(wc.at[q_me], wc.at[q_me], left))
        c_sib[layer].append(links.start(wc.at[q_me], wv.at[layer, 1, 1, q_me], sib))
    for layer in range(2):
        wc = wv.at[layer, 1, 0]
        links.arrived(c_r[layer], wc.at[q_left])
        c_fr.append(links.start(wc.at[halfq(me + 3, 0)], wc.at[halfq(me + 3, 0)], right))
        links.arrived(c_l[layer], wc.at[q_right])
        c_fl.append(links.start(wc.at[halfq(me + 1, 1)], wc.at[halfq(me + 1, 1)], left))
        c_sib[layer].append(links.start(wc.at[q_left], wv.at[layer, 1, 1, q_left], sib))
        c_sib[layer].append(links.start(wc.at[q_right], wv.at[layer, 1, 1, q_right], sib))

    def weights_done(layer):
        wc = wv.at[layer, 1, 0]
        links.arrived(c_fr[layer], wc.at[q_far0])
        links.arrived(c_fl[layer], wc.at[q_far1])
        q_far = quart(me + 2)
        c_sib[layer].append(links.start(wc.at[q_far], wv.at[layer, 1, 1, q_far], sib))
        links.arrived(c_sib[layer][0], wv.at[layer, 0, 1])
        for i, q in zip(c_sib[layer][1:], (q_me, q_left, q_right, q_far)):
            links.arrived(i, wv.at[layer, 1, 1, q])

    def tile(layer, k, cr, j, i):
        return wv[layer, k, cr, pl.ds(pl.multiple_of((2 * j + i) * TILE, TILE), TILE), :]

    def mixed(ref, layer, u):
        return ref[u] * live_s[layer, u] + ref[pair_s[layer, u]] * both_s[layer, u]

    def put(layer, k, cr, j, i, value):
        rows = pl.ds(pl.multiple_of((2 * j + i) * TILE, TILE), TILE)
        if cr == 0:
            gmine[layer, k, rows, :] = value
        else:
            gsend[layer, k, rows, :] = value.astype(bf16)

    groups = [(k, cr) for cr in (1, 0) for k in (0, 1)]

    def project(layer):
        def step(j, carry):
            for k, cr in groups:
                u = slot_of(k, cr, j)
                ct[u] = dot(xv[layer, u], tile(layer, k, cr, j, 0), 1, 0)
            return carry

        lax.fori_loop(0, per_owner, step, 0)

    def middle(layer):
        def step(j, carry):
            for k, cr in groups:
                u = slot_of(k, cr, j)
                value, slope = gelu_pair(mixed(ct, layer, u))
                sl[u] = slope
                active = value.astype(bf16)
                second = tile(layer, k, cr, j, 1)
                delta = dot(active, second, 1, 0)
                cotangent = (loss_scale * (xv[layer, u].astype(f32) + delta)).astype(bf16)
                sp[u] = dot(cotangent, second, 1, 1)
                put(layer, k, cr, j, 1, dot(active, cotangent, 0, 0))
            return carry

        lax.fori_loop(0, per_owner, step, 0)

    def last(layer, cr):
        def step(j, carry):
            for k in (0, 1):
                u = slot_of(k, cr, j)
                grad_pre = (mixed(sp, layer, u) * sl[u]).astype(bf16)
                put(layer, k, cr, j, 0, dot(xv[layer, u], grad_pre, 0, 0))
            return carry

        lax.fori_loop(0, per_owner, step, 0)

    c_g = {}

    def swap(layer):
        for k in range(2):
            c_g[layer, k] = links.start(gsend.at[layer, k], grecv.at[layer, k], sib)

    def join(layer):
        for k in range(2):
            links.arrived(c_g[layer, k], grecv.at[layer, k])

            def step(i, carry, k=k):
                rows = pl.ds(pl.multiple_of(i * chunk_rows, chunk_rows), chunk_rows)
                gsum[layer, k, rows, :] = (gmine[layer, k, rows, :] + grecv[layer, k, rows, :].astype(f32)).astype(bf16)
                return carry

            lax.fori_loop(0, nx, step, 0)

    def part(chunk, wave):
        return pl.ds(pl.multiple_of(lax.rem(chunk, nx) * chunk_rows + wave * sub, sub), sub)

    c_ring = {}
    ways = ((slots_p, right, 1), (slots_m, left, -1))

    def slot_at(d, layer, k, wave, t):
        return ways[d][0].at[layer, k, wave, t]

    def hop(layer, t, waves=range(WAVES)):
        for wave in waves:
            for d in range(2):
                for k in (d, 1 - d):
                    if t == 0 and k != d:
                        continue
                    chunk = part(me + ways[d][2] * (half - t) + nx, wave)
                    if t == 0 or (t == 1 and k != d):
                        src = gsum.at[layer, k, chunk]
                    else:
                        src = slot_at(d, layer, k, wave, t - 1)
                        links.arrived(c_ring[d, layer, k, wave, t - 1], src)
                        src[...] = (src[...].astype(f32) + gsum[layer, k, chunk, :].astype(f32)).astype(bf16)
                    c_ring[d, layer, k, wave, t] = links.start(src, slot_at(d, layer, k, wave, t), ways[d][1])

    c_far = {}

    def finish(layer, wave):
        for k in range(2):
            total = gsum[layer, k, part(me, wave), :].astype(f32)
            for d in range(2):
                src = slot_at(d, layer, k, wave, half - 1)
                links.arrived(c_ring[d, layer, k, wave, half - 1], src)
                total = total + src[...].astype(f32)
            if layer == 0 and k == 0:
                fin[wave] = total
                continue
            i = layer * 2 + k - 1
            ysend[i, wave] = total.astype(bf16)
            device = (y_far, y_same, y_cross)[i]
            c_far[i, wave] = links.start(ysend.at[i, wave], yrecv.at[i, wave], device)

    for load in loads:
        load.wait()
    weights_done(0)
    project(0)
    middle(0)
    last(0, 1)
    swap(0)
    last(0, 0)
    weights_done(1)
    join(0)
    hop(0, 0)
    project(1)
    hop(0, 1)
    middle(1)
    for t in range(2, half):
        hop(0, t)
    last(1, 1)
    swap(1)
    last(1, 0)
    join(1)
    hop(1, 0)
    for wave in range(WAVES):
        finish(0, wave)
    for t in range(1, half):
        hop(1, t)
    for wave in range(WAVES):
        finish(1, wave)

    c_out = {}
    for wave in range(WAVES):
        total = fin[wave]
        for i in range(3):
            links.arrived(c_far[i, wave], yrecv.at[i, wave])
            total = total + yrecv[i, wave].astype(f32)
        mine = part(me, wave)
        outv[mine, :] = total.astype(bf16)
        for d in range(2):
            c_out[d, wave, 1] = links.start(outv.at[mine], outv.at[mine], ways[d][1])
    for t in range(2, half + 1):
        for wave in range(WAVES):
            for d in range(2):
                got = part(me - ways[d][2] * (t - 1) + nx, wave)
                links.arrived(c_out[d, wave, t - 1], outv.at[got])
                if t < half or d == wave % 2:
                    c_out[d, wave, t] = links.start(outv.at[got], outv.at[got], ways[d][1])
    for wave in range(WAVES):
        d = wave % 2
        links.arrived(c_out[d, wave, half], outv.at[part(me + half, wave)])
    store = pltpu.make_async_copy(outv, out, lsem.at[2])
    store.start()
    links.drain()
    store.wait()


def solution(mesh):
    nx, ns = mesh.shape["dp"], mesh.shape["section"]

    def body(x_down, x_up, w_tiles, tile_rows, tile_cols, counts):
        rows, width = x_down.shape[2:]
        layers, per_owner = w_tiles.shape[1:3]
        slots = tile_rows.shape[2]
        big = per_owner * 2 * TILE
        loss_scale = float(2 * rows * nx * mesh.shape["fsdp"]) ** (-0.5)
        f32, bf16 = jnp.float32, jnp.bfloat16
        sub = big // nx // WAVES
        n = copies_of(nx)
        smem = pl.BlockSpec(memory_space=pltpu.SMEM)
        hbm = pl.BlockSpec(memory_space=pl.ANY)
        blocks = pl.pallas_call(
            pick,
            out_shape=jax.ShapeDtypeStruct((2, slots, rows, TILE), bf16),
            in_specs=[smem] + [hbm] * 2,
            out_specs=pl.BlockSpec(memory_space=pltpu.VMEM),
            scratch_shapes=[pltpu.SemaphoreType.DMA((2, slots))],
        )(tile_rows.reshape(2, slots), x_down.reshape(rows, width), x_up.reshape(rows, width))
        pair, live, other_live = slot_pairs(tile_cols.reshape(2, slots), counts.reshape(2, -1))
        total = pl.pallas_call(
            functools.partial(kernel, nx, ns, loss_scale),
            out_shape=jax.ShapeDtypeStruct((big, TILE), bf16),
            in_specs=[smem] * 3 + [hbm] * 2,
            out_specs=hbm,
            scratch_shapes=[
                pltpu.VMEM((2, slots, rows, TILE), bf16),
                pltpu.VMEM((2, 2, 2, big, TILE), bf16),
                pltpu.VMEM((slots, rows, TILE), f32),
                pltpu.VMEM((slots, rows, TILE), f32),
                pltpu.VMEM((slots, rows, TILE), f32),
                pltpu.VMEM((2, 2, big, TILE), f32),
                pltpu.VMEM((2, 2, big, TILE), bf16),
                pltpu.VMEM((2, 2, big, TILE), bf16),
                pltpu.VMEM((2, 2, big, TILE), bf16),
                pltpu.VMEM((2, 2, WAVES, nx // 2, sub, TILE), bf16),
                pltpu.VMEM((2, 2, WAVES, nx // 2, sub, TILE), bf16),
                pltpu.VMEM((3, WAVES, sub, TILE), bf16),
                pltpu.VMEM((3, WAVES, sub, TILE), bf16),
                pltpu.VMEM((WAVES, sub, TILE), f32),
                pltpu.VMEM((big, TILE), bf16),
                pltpu.SemaphoreType.DMA((3,)),
                pltpu.SemaphoreType.DMA((n,)),
                pltpu.SemaphoreType.DMA((n,)),
            ],
            compiler_params=pltpu.CompilerParams(collective_id=0, has_side_effects=True),
        )(
            pair, live.astype(f32), (live * other_live).astype(f32), blocks, w_tiles.reshape(layers, big, TILE),
        )
        return total.reshape(1, per_owner, 2, TILE, TILE)

    in_specs = (
        P("section", "dp", "fsdp", None),
        P("section", "dp", "fsdp", None),
        P("section", None, "fsdp", None, None, None),
        P("section", None, None),
        P("section", None, None),
        P("section", None, None),
    )
    out_specs = P("section", "fsdp", None, None, None)
    return jax.shard_map(body, mesh=mesh, in_specs=in_specs, out_specs=out_specs, check_vma=False)
```

time: 319 us -> 94.5 us (0.30)
  the two profiles are of different devices: /device:TPU:22 before, /device:TPU:2 now
where the time goes in v1:
time: 94.5 us; the launch traced here: 94.1 us
  Pallas kernels  87.2 us (92%)
  local copies, waits for them, and re-layouts  4.16 us (4%)
  other arithmetic  2.68 us (3%)
    pallas_call x1, Pallas kernels, body(): pl.pallas_call(functools.partial(kernel, nx, ns, loss_scale), out_shape=j...  83.8 us
    pallas_call x1, Pallas kernels, body(): pl.pallas_call(pick, out_shape=jax.ShapeDtypeStruct((2, slots, rows, TILE...  3.39 us

profile of v1, /device:TPU:2, one launch (start us, length us, event | category | flops | bytes accessed | tf_op | source)
XLA Modules:
  0.0 94.1 jit_solution(4552967874953409730)
XLA Ops:
  0.0 0.1 lt.27
  0.1 0.7 lt.30
  0.8 0.1 lt.31
  0.9 0.6 convert_convert_fusion
  1.5 0.8 copy.7
  2.3 1.5 %fusion.2 = (s32[2,20]{0,1:T(8,128)S(1)}, s32[2,20]{0,1:T(8,128)S(1)}) fusion(pred[20,20]{1,0:T(8,128)(4,1)S(1)} %iota_compare_fusion, s32[2,20]{1,0:T(2,128)S(1)} %convert_element_type.14, s32[2,20]{1,0:T(2,128)} %bitcast.12, s32[2,20]{0,1:T(8,128)S(1)} %copy.7), kind=kLoop, calls=%fused_computation.3 | loop fusion | flops 4720 | bytes 1200 | tf_op jit(solution)/shard_map/reduce_sum | solution.py:40
  3.8 0.1 copy.8
  3.9 0.6 select_convert_fusion.both_s
  4.5 0.7 copy.9.pair_s
  5.1 3.4 %shard_map.64.x = bf16[2,20,128,128]{3,2,1,0:T(8,128)(2,1)} custom-call(s32[2,20]{1,0:T(2,128)} %bitcast.13, bf16[128,6144]{1,0:T(8,128)(2,1)} %bitcast.7, bf16[128,6144]{1,0:T(8,128)(2,1)} %bitcast.8), custom_call_target="tpu_custom_call" | custom-call | tf_op jit(solution)/shard_map/pallas_call | solution.py:346
  8.5 83.8 %shard_map.65 = bf16[1280,128]{1,0:T(8,128)(2,1)} custom-call(s32[2,20]{1,0:T(2,128)} %copy.9.pair_s, f32[2,20]{1,0:T(2,128)} %get-tuple-element.7.live_s, f32[2,20]{1,0:T(2,128)} %select_convert_fusion.both_s, bf16[2,20,128,128]{3,2,1,0:T(8,128)(2,1)} %shard_map.64.x, bf16[2,1280,128]{2,1,0:T(8,128)(2,1)} %bitcast.10), custom_call_target="tpu_custom_call" | custom-call | tf_op jit(solution)/shard_map/pallas_call | solution.py:354
  92.4 1.7 %copy.11 = bf16[1,5,2,128,128]{4,3,2,1,0:T(8,128)(2,1)} copy(bf16[1,5,2,128,128]{4,3,2,1,0:T(8,128)(2,1)} %bitcast.9) | data formatting | bytes 655360
  (3 shorter events, 0.0 us)

commit v2 on v0

v2 whole, which is shorter than its diff:
```python
import functools
import math

import jax
import jax.numpy as jnp
from jax import lax
from jax.experimental import pallas as pl
from jax.experimental.pallas import tpu as pltpu
from jax.sharding import PartitionSpec as P

TILE = 128
MESH = pl.DeviceIdType.MESH

tanh_scale = math.sqrt(2.0 / math.pi)
cubic_coef = 0.044715


def gelu_pair(hidden):
    square = hidden * hidden
    inner = hidden * (tanh_scale + (tanh_scale * cubic_coef) * square)
    part = 0.5 + 0.5 * jnp.tanh(inner)
    value = hidden * part
    slope = part + value * (1.0 - part) * (2.0 * tanh_scale + (6.0 * tanh_scale * cubic_coef) * square)
    return value, slope


def dot(a, b, ca, cb):
    return lax.dot_general(a, b, (((ca,), (cb,)), ((), ())), preferred_element_type=jnp.float32)


def pairs(counts_s, cols, pair, live, both):
    f32 = jnp.float32
    slots = cols.shape[1]
    per_owner = slots // counts_s.shape[1]
    down = lax.broadcasted_iota(jnp.int32, (slots, slots), 0)
    along = lax.broadcasted_iota(jnp.int32, (slots, slots), 1)

    def alive(ids, layer):
        held = jnp.zeros_like(ids)
        for o in range(counts_s.shape[1]):
            held = jnp.where(ids >= o * per_owner, counts_s[layer, o] + o * per_owner, held)
        return (ids < held).astype(f32)

    for layer in range(2):
        row = cols[pl.ds(layer, 1), :].astype(f32)
        column = jnp.sum(jnp.where(down == along, row, 0.0), axis=1, keepdims=True)
        same = jnp.where((column == row) & (down != along), 1.0, 0.0)
        mine = alive(along, layer)
        pair[pl.ds(layer, 1), :] = jnp.sum(same * down.astype(f32), axis=0, keepdims=True).astype(jnp.int32)
        live[pl.ds(layer, 1), :] = mine[:1]
        both[pl.ds(layer, 1), :] = jnp.sum(same * alive(down, layer) * mine, axis=0, keepdims=True)


class Links:
    def __init__(self, send_sems, recv_sems):
        self.send_sems, self.recv_sems = send_sems, recv_sems
        self.started = []

    def start(self, src, dst, device):
        i = len(self.started)
        copy = pltpu.make_async_remote_copy(
            src_ref=src, dst_ref=dst, send_sem=self.send_sems.at[i], recv_sem=self.recv_sems.at[i],
            device_id=device, device_id_type=MESH,
        )
        copy.start()
        self.started.append((copy, device))
        return i

    def arrived(self, i, landing):
        device = self.started[i][1]
        pltpu.make_async_remote_copy(
            src_ref=landing, dst_ref=landing, send_sem=self.send_sems.at[i],
            recv_sem=self.recv_sems.at[i], device_id=device, device_id_type=MESH,
        ).wait_recv()

    def drain(self):
        for copy, _ in self.started:
            copy.wait_send()


COPIES = 2 * 10 + 4 + 4 * 8 + 6 + 14


def kernel(nx, ns, loss_scale, rows_s, pair_s, live_s, both_s, x_down, x_up, w, out,
           xv, wv, ct, sp, sl, gmine, gsend, grecv, gsum, near, far, direct, merged, ysend, yrecv, fin, outv,
           xsem, lsem, send_sems, recv_sems):
    f32, bf16 = jnp.float32, jnp.bfloat16
    per_owner = w.shape[1] // (2 * TILE)
    quarter = w.shape[1] // 4
    unit_rows = per_owner * TILE
    sub = unit_rows // nx

    me = lax.axis_index("dp")
    sec = lax.axis_index("section")
    own = lax.axis_index("fsdp")
    hi, core = own // 2, own % 2
    mirror = lax.rem(sec + ns // 2, ns)
    across = lax.rem(own + 2, 4)
    sib = {"fsdp": own + 1 - 2 * core}
    y_same = {"section": mirror}
    y_cross = {"section": mirror, "fsdp": across}
    y_far = {"fsdp": across}

    def along(by):
        return {"dp": lax.rem(me + by + nx, nx)}

    peers = [y_far, sib, y_cross, y_same] + [along(by) for by in range(1, nx)]

    def fetch(b, carry):
        at = pl.ds(pl.multiple_of(b * TILE, TILE), TILE)
        pltpu.make_async_copy(x_down.at[:, at], xv.at[0, b], xsem.at[0, b]).start()
        pltpu.make_async_copy(x_up.at[:, at], xv.at[1, b], xsem.at[1, b]).start()
        return carry

    def fetched(b, carry):
        at = pl.ds(pl.multiple_of(b * TILE, TILE), TILE)
        pltpu.make_async_copy(x_down.at[:, at], xv.at[0, b], xsem.at[0, b]).wait()
        pltpu.make_async_copy(x_up.at[:, at], xv.at[1, b], xsem.at[1, b]).wait()
        return carry

    barrier = pltpu.get_barrier_semaphore()
    for peer in peers:
        pl.semaphore_signal(barrier, inc=1, device_id=peer, device_id_type=MESH)
    load_w = pltpu.make_async_copy(w, wv.at[:, 0, 0], lsem.at[0])
    load_w.start()
    lax.fori_loop(0, xv.shape[1], fetch, 0)
    pl.semaphore_wait(barrier, len(peers))

    links = Links(send_sems, recv_sems)

    def quart(x):
        return pl.ds(pl.multiple_of(lax.rem(x, 4) * quarter, quarter), quarter)

    def halfq(x, second):
        return pl.ds(pl.multiple_of(lax.rem(x, 4) * quarter + second * (quarter // 2), quarter // 2), quarter // 2)

    q_me, q_left, q_right, q_far = quart(me), quart(me + 3), quart(me + 1), quart(me + 2)
    c_w = [{}, {}]
    for layer in range(2):
        c_w[layer]["y"] = links.start(w.at[layer, q_me], wv.at[layer, 1, 0, q_me], y_far)
    for layer in range(2):
        c_w[layer]["own"] = links.start(w.at[layer], wv.at[layer, 0, 1], sib)
    for layer in range(2):
        wc = wv.at[layer, 1, 0]
        links.arrived(c_w[layer]["y"], wc.at[q_me])
        for name, by, at in (("r", 1, q_me), ("l", -1, q_me), ("rr", 2, halfq(me, 0)), ("ll", -2, halfq(me, 1))):
            c_w[layer][name] = links.start(wc.at[at], wc.at[at], along(by))
        c_w[layer]["s_me"] = links.start(wc.at[q_me], wv.at[layer, 1, 1, q_me], sib)

    def pass_on(layer):
        wc = wv.at[layer, 1, 0]
        links.arrived(c_w[layer]["r"], wc.at[q_left])
        c_w[layer]["s_left"] = links.start(wc.at[q_left], wv.at[layer, 1, 1, q_left], sib)
        links.arrived(c_w[layer]["l"], wc.at[q_right])
        c_w[layer]["s_right"] = links.start(wc.at[q_right], wv.at[layer, 1, 1, q_right], sib)
        links.arrived(c_w[layer]["rr"], wc.at[halfq(me + 2, 0)])
        links.arrived(c_w[layer]["ll"], wc.at[halfq(me + 2, 1)])
        c_w[layer]["s_far"] = links.start(wc.at[q_far], wv.at[layer, 1, 1, q_far], sib)

    def weights_done(layer):
        links.arrived(c_w[layer]["own"], wv.at[layer, 0, 1])
        for name, q in (("s_me", q_me), ("s_left", q_left), ("s_right", q_right), ("s_far", q_far)):
            links.arrived(c_w[layer][name], wv.at[layer, 1, 1, q])

    def slot_of(k, cr, j):
        return (lax.rem(hi + k, 2) * 2 + lax.rem(core + cr, 2)) * per_owner + j

    def block(layer, u):
        return xv[layer, rows_s[layer, u]]

    def tile(layer, k, cr, j, i):
        return wv[layer, k, cr, pl.ds(pl.multiple_of((2 * j + i) * TILE, TILE), TILE), :]

    def mixed(ref, layer, u):
        return ref[u] * live_s[layer, u] + ref[pair_s[layer, u]] * both_s[layer, u]

    def put(layer, k, cr, j, i, value):
        rows = pl.ds(pl.multiple_of(j * TILE, TILE), TILE)
        if cr == 0:
            gmine[layer, i, k, rows, :] = value
        else:
            gsend[layer, i, k, rows, :] = value.astype(bf16)

    groups = [(k, cr) for cr in (1, 0) for k in (0, 1)]

    def project(layer):
        def step(j, carry):
            for k, cr in groups:
                u = slot_of(k, cr, j)
                ct[u] = dot(block(layer, u), tile(layer, k, cr, j, 0), 1, 0)
            return carry

        lax.fori_loop(0, per_owner, step, 0)

    def middle(layer):
        def step(j, carry):
            for k, cr in groups:
                u = slot_of(k, cr, j)
                value, slope = gelu_pair(mixed(ct, layer, u))
                sl[u] = slope
                active = value.astype(bf16)
                second = tile(layer, k, cr, j, 1)
                delta = dot(active, second, 1, 0)
                cotangent = (loss_scale * (block(layer, u).astype(f32) + delta)).astype(bf16)
                sp[u] = dot(cotangent, second, 1, 1)
                put(layer, k, cr, j, 1, dot(active, cotangent, 0, 0))
            return carry

        lax.fori_loop(0, per_owner, step, 0)

    def last(layer, cr):
        def step(j, carry):
            for k in (0, 1):
                u = slot_of(k, cr, j)
                grad_pre = (mixed(sp, layer, u) * sl[u]).astype(bf16)
                put(layer, k, cr, j, 0, dot(block(layer, u), grad_pre, 0, 0))
            return carry

        lax.fori_loop(0, per_owner, step, 0)

    c_g, c_t, c_far, c_out = {}, {}, {}, {}

    def swap(u):
        c_g[u] = links.start(gsend.at[u], grecv.at[u], sib)

    def join(u):
        links.arrived(c_g[u], grecv.at[u])

        def step(d, carry):
            rows = pl.ds(pl.multiple_of(d * sub, sub), sub)
            for k in range(2):
                gsum[(*u, d, k)] = (gmine[(*u, k, rows)] + grecv[(*u, k, rows)].astype(f32)).astype(bf16)
            return carry

        lax.fori_loop(0, nx, step, 0)

    def chunk(by):
        return lax.rem(me + by + nx, nx)

    def climb(u):
        for d, s in enumerate((1, -1)):
            c_t[u, d, "far"] = links.start(gsum.at[(*u, chunk(4 * s), d)], far.at[(d, *u)], along(2 * s))
            c_t[u, d, "near"] = links.start(gsum.at[(*u, chunk(3 * s))], near.at[(d, *u)], along(s))
        for d, s in enumerate((1, -1)):
            c_t[u, d, "direct"] = links.start(gsum.at[(*u, chunk(s))], direct.at[(d, *u)], along(s))

    def merge(u):
        for d, s in enumerate((1, -1)):
            links.arrived(c_t[u, d, "near"], near.at[(d, *u)])
            links.arrived(c_t[u, d, "far"], far.at[(d, *u)])
            for k in range(2):
                total = near[(d, *u, k)].astype(f32) + gsum[(*u, chunk(2 * s), k)].astype(f32)
                if k == d:
                    total = total + far[(d, *u)].astype(f32)
                near[(d, *u, k)] = total.astype(bf16)
            c_t[u, d, "merged"] = links.start(near.at[(d, *u)], merged.at[(d, *u)], along(2 * s))

    def finish(u):
        layer, i = u
        for d in range(2):
            links.arrived(c_t[u, d, "direct"], direct.at[(d, *u)])
            links.arrived(c_t[u, d, "merged"], merged.at[(d, *u)])
        for k in range(2):
            total = gsum[(*u, me, k)].astype(f32)
            for d in range(2):
                total = total + direct[(d, *u, k)].astype(f32) + merged[(d, *u, k)].astype(f32)
            if layer == 0 and k == 0:
                fin[i] = total
                continue
            y = layer * 2 + k - 1
            ysend[y, i] = total.astype(bf16)
            c_far[y, i] = links.start(ysend.at[y, i], yrecv.at[y, i], (y_far, y_same, y_cross)[y])

    def part(by):
        return pl.ds(pl.multiple_of(chunk(by) * sub, sub), sub)

    def share(i):
        total = fin[i]
        for y in range(3):
            links.arrived(c_far[y, i], yrecv.at[y, i])
            total = total + yrecv[y, i].astype(f32)
        outv[i, part(0), :] = total.astype(bf16)
        for by in (4, -3, 3, -2, 2, -1, 1):
            c_out[by, i] = links.start(outv.at[i, part(0)], outv.at[i, part(0)], along(by))

    stores = []

    def collect(i):
        for by in (-1, 1, -2, 2, -3, 3, 4):
            links.arrived(c_out[by, i], outv.at[i, part(-by)])
        for j in range(per_owner):
            rows = pl.ds((2 * j + i) * TILE, TILE)
            stores.append(pltpu.make_async_copy(outv.at[i, pl.ds(j * TILE, TILE)], out.at[rows], lsem.at[2 * j + i]))
            stores[-1].start()

    load_w.wait()
    lax.fori_loop(0, xv.shape[1], fetched, 0)
    pass_on(0)
    weights_done(0)
    project(0)
    middle(0)
    swap((0, 1))
    pass_on(1)
    last(0, 1)
    swap((0, 0))
    last(0, 0)
    join((0, 1))
    climb((0, 1))
    weights_done(1)
    project(1)
    join((0, 0))
    climb((0, 0))
    merge((0, 1))
    middle(1)
    swap((1, 1))
    merge((0, 0))
    finish((0, 1))
    last(1, 1)
    swap((1, 0))
    last(1, 0)
    join((1, 1))
    climb((1, 1))
    finish((0, 0))
    join((1, 0))
    climb((1, 0))
    merge((1, 1))
    merge((1, 0))
    finish((1, 1))
    finish((1, 0))
    share(1)
    share(0)
    collect(1)
    collect(0)
    links.drain()
    for store in stores:
        store.wait()


def solution(mesh):
    nx, ns = mesh.shape["dp"], mesh.shape["section"]

    def body(x_down, x_up, w_tiles, tile_rows, tile_cols, counts):
        rows, width = x_down.shape[2:]
        layers, per_owner = w_tiles.shape[1:3]
        slots = tile_rows.shape[2]
        unit = per_owner * TILE
        sub = unit // nx
        loss_scale = float(2 * rows * nx * mesh.shape["fsdp"]) ** (-0.5)
        f32, bf16 = jnp.float32, jnp.bfloat16
        smem = pl.BlockSpec(memory_space=pltpu.SMEM)
        vmem = pl.BlockSpec(memory_space=pltpu.VMEM)
        hbm = pl.BlockSpec(memory_space=pl.ANY)
        table = jax.ShapeDtypeStruct((2, slots), f32)
        pair, live, both = pl.pallas_call(
            pairs,
            out_shape=(jax.ShapeDtypeStruct((2, slots), jnp.int32), table, table),
            in_specs=[smem, vmem],
            out_specs=(vmem, vmem, vmem),
        )(counts.reshape(2, -1), tile_cols.reshape(2, slots))
        total = pl.pallas_call(
            functools.partial(kernel, nx, ns, loss_scale),
            out_shape=jax.ShapeDtypeStruct((2 * unit, TILE), bf16),
            in_specs=[smem] * 4 + [hbm] * 3,
            out_specs=hbm,
            scratch_shapes=[
                pltpu.VMEM((2, width // TILE, rows, TILE), bf16),
                pltpu.VMEM((2, 2, 2, 2 * unit, TILE), bf16),
                pltpu.VMEM((slots, rows, TILE), f32),
                pltpu.VMEM((slots, rows, TILE), f32),
                pltpu.VMEM((slots, rows, TILE), f32),
                pltpu.VMEM((2, 2, 2, unit, TILE), f32),
                pltpu.VMEM((2, 2, 2, unit, TILE), bf16),
                pltpu.VMEM((2, 2, 2, unit, TILE), bf16),
                pltpu.VMEM((2, 2, nx, 2, sub, TILE), bf16),
                pltpu.VMEM((2, 2, 2, 2, sub, TILE), bf16),
                pltpu.VMEM((2, 2, 2, sub, TILE), bf16),
                pltpu.VMEM((2, 2, 2, 2, sub, TILE), bf16),
                pltpu.VMEM((2, 2, 2, 2, sub, TILE), bf16),
                pltpu.VMEM((3, 2, sub, TILE), bf16),
                pltpu.VMEM((3, 2, sub, TILE), bf16),
                pltpu.VMEM((2, sub, TILE), f32),
                pltpu.VMEM((2, unit, TILE), bf16),
                pltpu.SemaphoreType.DMA((2, width // TILE)),
                pltpu.SemaphoreType.DMA((2 * per_owner,)),
                pltpu.SemaphoreType.DMA((COPIES,)),
                pltpu.SemaphoreType.DMA((COPIES,)),
            ],
            compiler_params=pltpu.CompilerParams(collective_id=0, has_side_effects=True),
        )(
            tile_rows.reshape(2, slots), pair, live, both,
            x_down.reshape(rows, width), x_up.reshape(rows, width), w_tiles.reshape(layers, 2 * unit, TILE),
        )
        return total.reshape(1, per_owner, 2, TILE, TILE)

    in_specs = (
        P("section", "dp", "fsdp", None),
        P("section", "dp", "fsdp", None),
        P("section", None, "fsdp", None, None, None),
        P("section", None, None),
        P("section", None, None),
        P("section", None, None),
    )
    out_specs = P("section", "fsdp", None, None, None)
    return jax.shard_map(body, mesh=mesh, in_specs=in_specs, out_specs=out_specs, check_vma=False)
```

time: 319 us -> 75.3 us (0.24)
  the two profiles are of different devices: /device:TPU:22 before, /device:TPU:2 now
where the time goes in v2:
time: 75.3 us; the launch traced here: 75.1 us
  Pallas kernels  73.4 us (97%)
  local copies, waits for them, and re-layouts  1.72 us (2%)
    pallas_call x1, Pallas kernels, body(): pl.pallas_call(functools.partial(kernel, nx, ns, loss_scale), out_shape=j...  72.1 us
    unnamed x1, local copies, waits for them, and re-layouts  1.72 us

profile of v2, /device:TPU:2, one launch (start us, length us, event | category | flops | bytes accessed | tf_op | source)
XLA Modules:
  0.0 75.1 jit_solution(5030531114801009668)
XLA Ops:
  0.0 1.4 %shard_map.64 = (s32[2,20]{1,0:T(2,128)}, f32[2,20]{1,0:T(2,128)}, f32[2,20]{1,0:T(2,128)}) custom-call(s32[2,4]{1,0:T(2,128)} %bitcast.12, s32[2,20]{1,0:T(2,128)} %bitcast.13), custom_call_target="tpu_custom_call" | custom-call | tf_op jit(solution)/shard_map/pallas_call | solution.py:354
  1.4 72.1 %shard_map.65 = bf16[1280,128]{1,0:T(8,128)(2,1)} custom-call(s32[2,20]{1,0:T(2,128)} %bitcast.11, s32[2,20]{1,0:T(2,128)} %get-tuple-element.8.pair_s, f32[2,20]{1,0:T(2,128)} %get-tuple-element.9.live_s, f32[2,20]{1,0:T(2,128)} %get-tuple-element.10.both_s, bf16[128,6144]{1,0:T(8,128)(2,1)} %bitcast.7, bf16[128,6144]{1,0:T(8,128)(2,1)} %bitcast.8, ...), custom_call_target="tpu_custom_call" | custom-call | tf_op jit(solution)/shard_map/pallas_call | solution.py:360
  73.4 1.7 %copy.8 = bf16[1,5,2,128,128]{4,3,2,1,0:T(8,128)(2,1)} copy(bf16[1,5,2,128,128]{4,3,2,1,0:T(8,128)(2,1)} %bitcast.9) | data formatting | bytes 655360
